TPU v7x, 32 devices: a whole 2x2x4 slice. The times are simulated.
32 devices in a mesh: gz: 4 (over y, x), gy: 2 (over core), gx: 4 (over z).
Axes of the slice: x: 2, y: 2, z: 4, core: 2. Of those that a mesh axis runs over, the one named last changes fastest.
Arguments:
- populations: float32 [19, 32, 16, 512], P(None, 'gz', 'gy', 'gx'), may hold values from 0.1 to 20, as said below
- solid: int32 [32, 16, 512], P('gz', 'gy', 'gx'), may hold values 0 or 1
- ports: int32 [2, 16, 512], P(None, 'gy', 'gx'), may hold values 0 or 1
- concentration: float32 [2, 4, 2, 64], P(None, 'gz'), may hold values from 0 to 1
- loaded: float32 [2, 4, 2, 64], P(None, 'gz'), may hold values from 0 to 2
Outputs:
- final_populations: float32 [19, 32, 16, 512], P(None, 'gz', 'gy', 'gx')
- new_concentration: float32 [2, 4, 2, 64], P(None, 'gz')
- new_loaded: float32 [2, 4, 2, 64], P(None, 'gz')
Inputs may be any that keep to these rules, and one draw needn't show every extreme that they name: `populations`: every population is positive and of the size of its lattice weight times 36.
All inputs are finite; a program needn't handle non-finite values. No bound on the sum of `solid` or of `ports` on one device may be relied on, other than what follows from the above.
Results may differ from a plain program's by a relative error of at most 0.00002.
Values sent between devices are 32-bit elements; how exact they have to be, the bound alone decides.
A program may use at most 64 MiB of HBM per device.

v0:
```python
import jax
import jax.numpy as jnp
from jax import lax
from jax.sharding import PartitionSpec as P

ITERS = 2


lattice = [
    (0, 0, 0),
    (1, 0, 0),
    (-1, 0, 0),
    (0, 1, 0),
    (0, -1, 0),
    (0, 0, 1),
    (0, 0, -1),
    (1, 1, 0),
    (-1, -1, 0),
    (1, -1, 0),
    (-1, 1, 0),
    (1, 0, 1),
    (-1, 0, -1),
    (1, 0, -1),
    (-1, 0, 1),
    (0, 1, 1),
    (0, -1, -1),
    (0, 1, -1),
    (0, -1, 1),
]
opposite = [0, 2, 1, 4, 3, 6, 5, 8, 7, 10, 9, 12, 11, 14, 13, 16, 15, 18, 17]
weights = [1.0 / 3.0] + [1.0 / 18.0] * 6 + [1.0 / 36.0] * 12
relax_rate = 1.25
base_density = 36.0
inlet_speed = 0.05
spread_base = (0.03, 0.06)
spread_length = 0.1
uptake_rate = (0.3, 0.6)
affinity = (2.0, 0.5)
phase_ratio = 0.5
feed_level = (1.0, 0.5)


def extended(cells, sides, width, closed):
    for axis, dim in sides:
        count = lax.axis_size(axis)
        ends = count if closed else count - 1
        head = lax.slice_in_dim(cells, 0, width, axis=dim)
        tail = lax.slice_in_dim(cells, cells.shape[dim] - width, cells.shape[dim], axis=dim)
        cells = jnp.concatenate(
            [
                lax.ppermute(tail, axis, [(i, (i + 1) % count) for i in range(ends)]),
                cells,
                lax.ppermute(head, axis, [((i + 1) % count, i) for i in range(ends)]),
            ],
            axis=dim,
        )
    return cells


def equilibrium(density, velocity):
    speed_z, speed_y, speed_x = velocity
    square = speed_z * speed_z + speed_y * speed_y + speed_x * speed_x
    result = []
    for member in range(19):
        step_z, step_y, step_x = lattice[member]
        along = step_z * speed_z + step_y * speed_y + step_x * speed_x
        result.append(
            weights[member] * density * (1.0 + 3.0 * along + 4.5 * along * along - 1.5 * square)
        )
    return result


def moments(pops):
    density = pops[0]
    for member in range(1, 19):
        density = density + pops[member]
    flows = []
    for position in range(3):
        total = jnp.zeros_like(pops[0])
        for member in range(19):
            heading = lattice[member][position]
            if heading == 1:
                total = total + pops[member]
            elif heading == -1:
                total = total - pops[member]
        flows.append(total)
    return (density, flows)


def collide(pops, solid_flag):
    density, flows = moments(pops)
    velocity = [flow / density for flow in flows]
    balance = equilibrium(density, velocity)
    post = [
        jnp.where(
            solid_flag,
            pops[opposite[member]],
            pops[member] - relax_rate * (pops[member] - balance[member]),
        )
        for member in range(19)
    ]
    return (post, velocity)


def close_ends(moved, post, velocity, ports, first_dev, last_dev):
    inflow = equilibrium(base_density, (inlet_speed, 0.0, 0.0))
    outflow = equilibrium(base_density, (velocity[0][-1], velocity[1][-1], velocity[2][-1]))
    inlet_open = ports[0] == 1
    outlet_open = ports[1] == 1
    result = list(moved)
    for member in range(19):
        step_z = lattice[member][0]
        back = post[opposite[member]]
        if step_z == 1:
            entering = jnp.where(inlet_open, inflow[member], back[0])
            result[member] = (
                result[member].at[0].set(jnp.where(first_dev, entering, result[member][0]))
            )
        elif step_z == -1:
            entering = jnp.where(outlet_open, outflow[member], back[-1])
            result[member] = (
                result[member].at[-1].set(jnp.where(last_dev, entering, result[member][-1]))
            )
    return result


def block_sum(field):
    depth, height, width = field.shape
    return field.reshape(depth // 8, 8, height // 8, 8, width // 8, 8).sum(axis=(1, 3, 5))


def transport(padded, loaded, coarse_vel):
    centre = padded[:, 1:-1]
    neighbours = [
        (padded[:, :-2], padded[:, 2:]),
        (jnp.roll(centre, 1, axis=2), jnp.roll(centre, -1, axis=2)),
        (jnp.roll(centre, 1, axis=3), jnp.roll(centre, -1, axis=3)),
    ]
    change = jnp.zeros_like(centre)
    curvature = jnp.zeros_like(centre)
    reach = jnp.zeros_like(coarse_vel[0])
    for direction in range(3):
        courant = 8.0 * coarse_vel[direction]
        before, after = neighbours[direction]
        change = (
            change
            - jnp.maximum(courant, 0.0) * (centre - before)
            - jnp.minimum(courant, 0.0) * (after - centre)
        )
        curvature = curvature + after - 2.0 * centre + before
        reach = reach + jnp.abs(courant)
    base = jnp.array(spread_base, dtype=centre.dtype)[:, None, None, None]
    speed = jnp.array(uptake_rate, dtype=centre.dtype)[:, None, None, None]
    holding = jnp.array(affinity, dtype=centre.dtype)[:, None, None, None]
    rate = speed * (holding * centre - loaded)
    new_conc = centre + change + (base + spread_length * reach) * curvature - phase_ratio * rate
    return (new_conc, loaded + rate)


def body(populations, solid, ports, concentration, loaded):
    depth, height, width = solid.shape
    slab_pos = lax.axis_index("gz")
    first_dev = slab_pos == 0
    last_dev = slab_pos == lax.axis_size("gz") - 1
    pops = [populations[member] for member in range(19)]
    solid_flag = solid == 1
    for iteration in range(ITERS):
        post, velocity = collide(pops, solid_flag)
        padded = extended(jnp.stack(post), (("gz", 1), ("gy", 2), ("gx", 3)), 1, True)
        moved = []
        for member in range(19):
            step_z, step_y, step_x = lattice[member]
            moved.append(
                padded[
                    member,
                    1 - step_z : 1 - step_z + depth,
                    1 - step_y : 1 - step_y + height,
                    1 - step_x : 1 - step_x + width,
                ]
            )
        pops = close_ends(moved, post, velocity, ports, first_dev, last_dev)
    final = jnp.stack(pops)
    density, flows = moments(pops)
    fluid = (solid == 0).astype(jnp.float32)
    local = jnp.stack([block_sum(flow * fluid) for flow in flows]) / (512.0 * base_density)
    across = lax.all_gather(local, "gy", axis=2, tiled=True)
    coarse_vel = lax.all_gather(across, "gx", axis=3, tiled=True)
    padded_conc = extended(concentration, (("gz", 1),), 1, False)
    feed = jnp.broadcast_to(
        jnp.array(feed_level, dtype=jnp.float32)[:, None, None],
        (2, concentration.shape[2], concentration.shape[3]),
    )
    front = jnp.where(first_dev, feed, padded_conc[:, 0])
    rear = jnp.where(last_dev, concentration[:, -1], padded_conc[:, -1])
    padded_conc = padded_conc.at[:, 0].set(front).at[:, -1].set(rear)
    new_conc, new_load = transport(padded_conc, loaded, coarse_vel)
    return (final, new_conc, new_load)


def solution(mesh):
    placed = (
        P(None, "gz", "gy", "gx"),
        P("gz", "gy", "gx"),
        P(None, "gy", "gx"),
        P(None, "gz", None, None),
        P(None, "gz", None, None),
    )
    return jax.shard_map(
        body,
        mesh=mesh,
        in_specs=placed,
        out_specs=(P(None, "gz", "gy", "gx"), P(None, "gz", None, None), P(None, "gz", None, None)),
        check_vma=False,
    )
```

profile of v0, /device:TPU:0, one launch (start us, length us, event | category | flops | bytes accessed | tf_op | source)
XLA Modules:
  0.0 104.6 jit_solution(4216951791328130897)
XLA Ops:
  0.6 5.6 %collective-permute-start.12 = (f32[2,1,2,64]{3,2,1,0:T(2,128)}, f32[2,1,2,64]{3,2,1,0:T(2,128)}, u32[]{:S(2)}, u32[]{:S(2)}) collective-permute-start(f32[2,1,2,64]{3,2,1,0:T(2,128)} %param.56), channel_id=1, source_target_pairs={{0,8},{8,16},{16,24},{1,9},{9,17},{17,25},{2,10},{10,18},{18,26},{... | collective-permute-start | bytes 3080 | tf_op jit(solution)/shard_map/ppermute | solution.py:51
  6.2 1.3 %collective-permute-start.13 = (f32[2,1,2,64]{3,2,1,0:T(2,128)}, f32[2,1,2,64]{3,2,1,0:T(2,128)}, u32[]{:S(2)}, u32[]{:S(2)}) collective-permute-start(f32[2,1,2,64]{3,2,1,0:T(2,128)} %param.56), channel_id=1, source_target_pairs={{8,0},{16,8},{24,16},{9,1},{17,9},{25,17},{10,2},{18,10},{26,18},{... | collective-permute-start | bytes 3080 | tf_op jit(solution)/shard_map/ppermute | solution.py:53
  7.5 1.2 %constant_dynamic-update-slice_fusion.18 = (f32[19,8,8,128]{3,2,1,0:T(8,128)S(1)}, f32[8,8,128]{2,1,0:T(8,128)S(1)}, f32[8,8,128]{2,1,0:T(8,128)S(1)}, f32[8,8,1...) fusion(f32[19,8,8,128]{3,2,1,0:T(8,128)} %param.53, ...), kind=kLoop, calls=%fused_computation.20 | loop fusion | flops 589823 | bytes 860160
  8.7 0.8 constant_dynamic-update-slice_fusion.17
  9.5 0.8 constant_dynamic-update-slice_fusion.16
  10.3 0.8 constant_dynamic-update-slice_fusion.15
  11.8 2.7 %collective-permute-start = (f32[19,1,8,128]{3,2,1,0:T(8,128)S(1)}, f32[19,1,8,128]{3,2,1,0:T(8,128)S(1)}, u32[]{:S(2)}, u32[]{:S(2)}) collective-permute-start(f32[19,1,8,128]{3,2,1,0:T(8,128)S(1)} %get-tuple-element.383), channel_id=1, source_target_pairs={{0,8},{8,16},{16,24},{24,0},{1,9},{9,17},{17,25},{25,1},{2,10},{10... | collective-permute-start | bytes 233480 | tf_op jit(solution)/shard_map/ppermute | solution.py:51
  14.5 1.0 collective-permute-start.1
  15.6 0.7 fusion.359
  16.2 2.4 %collective-permute-done = f32[19,1,8,128]{3,2,1,0:T(8,128)S(1)} collective-permute-done((f32[19,1,8,128]{3,2,1,0:T(8,128)S(1)}, f32[19,1,8,128]{3,2,1,0:T(8,128)S(1)}, u32[]{:S(2)}, u32[]{:S(2)}) %collective-permute-start) | collective-permute-done | bytes 77856 | tf_op jit(solution)/shard_map/ppermute | solution.py:51
  18.6 0.9 collective-permute-done.1
  20.3 0.7 fusion.391
  21.5 1.7 %fusion.386 = (f32[19,10,10,1]{3,2,1,0:T(8,128)}, f32[19,10,10,1]{3,2,1,0:T(8,128)S(1)}) fusion(f32[19,10,10,128]{3,2,1,0:T(8,128)S(1)} %pad_maximum_fusion), kind=kLoop, calls=%fused_computation.679 | loop fusion | bytes 30400 | tf_op jit(solution)/shard_map/slice | solution.py:47
  23.2 2.1 %copy.55 = f32[19,10,10,1]{0,3,2,1:T(1,128)S(1)} copy(f32[19,10,10,1]{3,2,1,0:T(8,128)} %get-tuple-element.355) | data formatting | bytes 15200 | tf_op jit(solution)/shard_map/slice | solution.py:47
  25.4 3.6 %collective-permute-start.5 = (f32[19,10,10,1]{0,3,2,1:T(1,128)S(1)}, f32[19,10,10,1]{0,3,2,1:T(1,128)S(1)}, u32[]{:S(2)}, u32[]{:S(2)}) collective-permute-start(f32[19,10,10,1]{0,3,2,1:T(1,128)S(1)} %copy.55), channel_id=1, source_target_pairs={{1,0},{2,1},{3,2},{0,3},{5,4},{6,5},{7,6},{4,7},{9,8},{10,9},{11,1... | collective-permute-start | bytes 22808 | tf_op jit(solution)/shard_map/ppermute | solution.py:53
  29.0 0.8 copy.53
  29.9 1.1 %collective-permute-done.5 = f32[19,10,10,1]{0,3,2,1:T(1,128)S(1)} collective-permute-done((f32[19,10,10,1]{0,3,2,1:T(1,128)S(1)}, f32[19,10,10,1]{0,3,2,1:T(1,128)S(1)}, u32[]{:S(2)}, u32[]{:S(2)}) %collective-permute-start.5) | collective-permute-done | bytes 7632 | tf_op jit(solution)/shard_map/ppermute | solution.py:53
  31.0 1.6 %copy.56 = f32[19,10,10,1]{3,2,1,0:T(8,128)S(1)} copy(f32[19,10,10,1]{0,3,2,1:T(1,128)S(1)} %collective-permute-done.5) | data formatting | bytes 15200 | tf_op jit(solution)/shard_map/ppermute | solution.py:53
  32.7 3.0 %collective-permute-done.4 = f32[19,10,10,1]{0,3,2,1:T(1,128)S(1)} collective-permute-done((f32[19,10,10,1]{0,3,2,1:T(1,128)S(1)}, f32[19,10,10,1]{0,3,2,1:T(1,128)S(1)}, u32[]{:S(2)}, u32[]{:S(2)}) %collective-permute-start.4) | collective-permute-done | bytes 7632 | tf_op jit(solution)/shard_map/ppermute | solution.py:51
  35.7 2.7 %copy.54 = f32[19,10,10,1]{3,2,1,0:T(8,128)} copy(f32[19,10,10,1]{0,3,2,1:T(1,128)S(1)} %collective-permute-done.4) | data formatting | bytes 15200 | tf_op jit(solution)/shard_map/ppermute | solution.py:51
  38.4 1.0 maximum_bitcast_fusion.13
  39.5 1.3 %copy-done = f32[19,10,10,1]{3,2,1,0:T(8,128)S(1)} copy-done((f32[19,10,10,1]{3,2,1,0:T(8,128)S(1)}, f32[19,10,10,1]{3,2,1,0:T(8,128)}, u32[]{:S(2)}) %copy-start) | copy-done | bytes 7624
  41.8 0.7 constant_dynamic-update-slice_fusion.36
  42.4 0.6 constant_dynamic-update-slice_fusion.35
  43.2 0.6 constant_dynamic-update-slice_fusion.30
  43.9 0.6 constant_dynamic-update-slice_fusion.29
  44.5 0.6 constant_dynamic-update-slice_fusion.28
  45.1 0.6 constant_dynamic-update-slice_fusion.27
  45.8 0.6 constant_dynamic-update-slice_fusion.26
  46.4 0.6 constant_dynamic-update-slice_fusion.25
  47.0 0.6 constant_dynamic-update-slice_fusion.24
  47.7 0.6 constant_dynamic-update-slice_fusion.23
  48.5 2.1 %collective-permute-start.6 = (f32[19,1,8,128]{3,2,1,0:T(8,128)S(1)}, f32[19,1,8,128]{3,2,1,0:T(8,128)S(1)}, u32[]{:S(2)}, u32[]{:S(2)}) collective-permute-start(f32[19,1,8,128]{3,2,1,0:T(8,128)S(1)} %get-tuple-element.382), channel_id=1, source_target_pairs={{0,8},{8,16},{16,24},{24,0},{1,9},{9,17},{17,25},{25,1},{2,10},{10... | collective-permute-start | bytes 233480 | tf_op jit(solution)/shard_map/ppermute | solution.py:51
  50.6 0.8 collective-permute-start.7
  51.5 0.7 fusion.392
  52.1 1.7 %collective-permute-done.6 = f32[19,1,8,128]{3,2,1,0:T(8,128)S(1)} collective-permute-done((f32[19,1,8,128]{3,2,1,0:T(8,128)S(1)}, f32[19,1,8,128]{3,2,1,0:T(8,128)S(1)}, u32[]{:S(2)}, u32[]{:S(2)}) %collective-permute-start.6) | collective-permute-done | bytes 77856 | tf_op jit(solution)/shard_map/ppermute | solution.py:51
  53.8 1.2 %collective-permute-done.7 = f32[19,1,8,128]{3,2,1,0:T(8,128)S(1)} collective-permute-done((f32[19,1,8,128]{3,2,1,0:T(8,128)S(1)}, f32[19,1,8,128]{3,2,1,0:T(8,128)S(1)}, u32[]{:S(2)}, u32[]{:S(2)}) %collective-permute-start.7) | collective-permute-done | bytes 77856 | tf_op jit(solution)/shard_map/ppermute | solution.py:53
  55.7 0.6 fusion.390
  57.0 1.7 %fusion.385 = (f32[19,10,10,1]{3,2,1,0:T(8,128)S(1)}, f32[19,10,10,1]{3,2,1,0:T(8,128)}) fusion(f32[19,10,10,128]{3,2,1,0:T(8,128)S(1)} %pad_maximum_fusion.1), kind=kLoop, calls=%fused_computation.678 | loop fusion | bytes 30400 | tf_op jit(solution)/shard_map/slice | solution.py:47
  58.7 2.1 %copy.57 = f32[19,10,10,1]{0,3,2,1:T(1,128)S(1)} copy(f32[19,10,10,1]{3,2,1,0:T(8,128)} %get-tuple-element.354) | data formatting | bytes 15200 | tf_op jit(solution)/shard_map/slice | solution.py:48
  60.9 0.8 copy.59
  61.6 4.0 %collective-permute-start.11 = (f32[19,10,10,1]{0,3,2,1:T(1,128)S(1)}, f32[19,10,10,1]{0,3,2,1:T(1,128)}, u32[]{:S(2)}, u32[]{:S(2)}) collective-permute-start(f32[19,10,10,1]{0,3,2,1:T(1,128)S(1)} %copy.59), channel_id=1, source_target_pairs={{1,0},{2,1},{3,2},{0,3},{5,4},{6,5},{7,6},{4,7},{9,8},{10,9},{11,1... | collective-permute-start | bytes 22808 | tf_op jit(solution)/shard_map/ppermute | solution.py:53
  65.7 1.7 %collective-permute-done.11 = f32[19,10,10,1]{0,3,2,1:T(1,128)} collective-permute-done((f32[19,10,10,1]{0,3,2,1:T(1,128)S(1)}, f32[19,10,10,1]{0,3,2,1:T(1,128)}, u32[]{:S(2)}, u32[]{:S(2)}) %collective-permute-start.11) | collective-permute-done | bytes 7632 | tf_op jit(solution)/shard_map/ppermute | solution.py:53
  67.4 2.4 %copy.60 = f32[19,10,10,1]{3,2,1,0:T(8,128)S(1)} copy(f32[19,10,10,1]{0,3,2,1:T(1,128)} %collective-permute-done.11) | data formatting | bytes 15200 | tf_op jit(solution)/shard_map/ppermute | solution.py:53
  70.0 0.5 copy-done.13
  70.5 0.7 constant_dynamic-update-slice_fusion.64
  71.3 0.6 copy-done.4
  71.8 3.4 %copy.58 = f32[19,10,10,1]{3,2,1,0:T(8,128)} copy(f32[19,10,10,1]{0,3,2,1:T(1,128)} %collective-permute-done.10) | data formatting | bytes 15200 | tf_op jit(solution)/shard_map/ppermute | solution.py:51
  75.3 1.1 %maximum_bitcast_fusion.3 = (f32[8,8,128]{2,1,0:T(8,128)S(1)}, f32[8,8,128]{2,1,0:T(8,128)S(1)}, f32[8,8,128]{2,1,0:T(8,128)S(1)}) fusion(f32[19,10,10,1]{3,2,1,0:T(8,128)} %copy.58, f32[19,10,1,128]{3,2,1,0:T(1,128)S(1)} %collective-permute-done.9, f32[19,10,1,128]{3,2,1,0:T(1,128)S(1)} %collective-permute-done.8, ...), kind=kLoop, calls=%fused_computation.399 | loop fusion | flops 106496 | bytes 1078704 | tf_op jit(solution)/shard_map/squeeze | solution.py:174
  76.7 0.8 constant_dynamic-update-slice_fusion.57
  77.5 0.7 constant_dynamic-update-slice_fusion.61
  78.2 0.7 constant_dynamic-update-slice_fusion.59
  78.9 0.8 constant_dynamic-update-slice_fusion.60
  79.7 0.7 constant_dynamic-update-slice_fusion.63
  80.5 1.4 %select_reduce_fusion = (f32[128]{0:T(128)}, f32[128]{0:T(128)S(1)}, f32[128]{0:T(128)}, f32[1,8,8,128]{3,2,1,0:T(8,128)S(1)}, f32[1,8,8,128]{3,2,1,0:T(8,128)S(...) fusion(f32[8,8,128]{2,1,0:T(8,128)S(1)} %get-tuple-element.278,, ...), kind=kLoop, calls=%fused_computation.509 | loop fusion | flops 573056 | bytes 1612128 | tf_op jit(solution)/shard_map/reduce_sum | solution.py:129
  81.9 0.7 reduce_sum.37
  82.7 0.7 reduce_sum.40
  83.9 1.8 %all_gather.6 = f32[3,1,2,16]{3,1,0,2:T(1,128)S(1)} all-gather(f32[3,1,1,16]{3,1,0,2:T(1,128)S(1)} %fusion.358), channel_id=1, replica_groups=mesh['gz'=4,'gy'=2,'gx'=4] {'gy'}, dimensions={2}, use_global_device_ids=true | all-gather | bytes 576 | tf_op jit(solution)/shard_map/all_gather | solution.py:186
  85.8 13.6 %all_gather.7 = f32[3,1,2,64]{0,2,1,3:T(2,128)S(1)} all-gather(f32[3,1,2,16]{0,2,1,3:T(2,128)S(1)} %copy.62), channel_id=1, replica_groups=mesh['gz'=4,'gy'=2,'gx'=4] {'gx'}, dimensions={3}, use_global_device_ids=true | all-gather | bytes 1920 | tf_op jit(solution)/shard_map/all_gather | solution.py:187
  99.9 0.8 constant_dynamic-update-slice_fusion.53
  100.7 0.8 constant_dynamic-update-slice_fusion.52
  101.4 0.8 constant_dynamic-update-slice_fusion.51
  102.2 0.8 constant_dynamic-update-slice_fusion.50
  103.3 1.4 %multiply_subtract_fusion = f32[2,1,2,64]{3,2,1,0:T(2,128)} fusion(f32[2,1,2,64]{3,2,1,0:T(2,128)S(1)} %copy-done.9, f32[2,1,2,1]{3,2,1,0:T(2,128)S(1)} %copy-done.19, f32[2,1,2,63]{3,2,1,0:T(2,128)S(1)} %copy-done.21, f32[2,1,2,63]{3,2,1,0:T(2,128)S(1)} %copy-done.20, f32[2,1,2,1]{3,2,1,0:T(2,128)S(1)} %copy-done.18, f32[2,1,1,64]{3,2,1,0:T(1,128)S(1)} %copy-done.23, ...), kind=kLoop, calls=%fused_computation.666 | loop fusion | flops 10496 | bytes 11810 | tf_op jit(solution)/shard_map/sub | solution.py:156
  (138 shorter events, 6.6 us)
Async XLA Ops:
  0.6 10.5 %copy-start.2 = (f32[19,8,8,128]{3,2,1,0:T(8,128)S(1)}, f32[19,8,8,128]{3,2,1,0:T(8,128)}, u32[]{:S(2)}) copy-start(f32[19,8,8,128]{3,2,1,0:T(8,128)} %param.53) | copy-start | bytes 1867780
  0.6 102.5 %collective-permute-start.12 = (f32[2,1,2,64]{3,2,1,0:T(2,128)}, f32[2,1,2,64]{3,2,1,0:T(2,128)}, u32[]{:S(2)}, u32[]{:S(2)}) collective-permute-start(f32[2,1,2,64]{3,2,1,0:T(2,128)} %param.56), channel_id=1, source_target_pairs={{0,8},{8,16},{16,24},{1,9},{9,17},{17,25},{2,10},{10,18},{18,26},{... | collective-permute-start | bytes 3080 | tf_op jit(solution)/shard_map/ppermute | solution.py:51
  6.2 96.9 %collective-permute-start.13 = (f32[2,1,2,64]{3,2,1,0:T(2,128)}, f32[2,1,2,64]{3,2,1,0:T(2,128)}, u32[]{:S(2)}, u32[]{:S(2)}) collective-permute-start(f32[2,1,2,64]{3,2,1,0:T(2,128)} %param.56), channel_id=1, source_target_pairs={{8,0},{16,8},{24,16},{9,1},{17,9},{25,17},{10,2},{18,10},{26,18},{... | collective-permute-start | bytes 3080 | tf_op jit(solution)/shard_map/ppermute | solution.py:53
  11.3 4.3 %copy-start.8 = (f32[2,1,2,64]{3,2,1,0:T(2,128)S(1)}, f32[2,1,2,64]{3,2,1,0:T(2,128)}, u32[]{:S(2)}) copy-start(f32[2,1,2,64]{3,2,1,0:T(2,128)} %param.56) | copy-start | bytes 3076
  11.3 4.2 %copy-start.16 = (f32[2,1,2,64]{3,2,1,0:T(2,128)S(1)}, f32[2,1,2,64]{3,2,1,0:T(2,128)}, u32[]{:S(2)}) copy-start(f32[2,1,2,64]{3,2,1,0:T(2,128)} %param.57) | copy-start | bytes 3076
  11.3 4.2 %copy-start.24 = (f32[2]{0:T(128)S(1)}, f32[2]{0:T(128)}, u32[]{:S(2)}) copy-start(f32[2]{0:T(128)} %constant.557.clone) | copy-start | bytes 28
  11.3 4.2 %copy-start.26 = (f32[2]{0:T(128)S(1)}, f32[2]{0:T(128)}, u32[]{:S(2)}) copy-start(f32[2]{0:T(128)} %constant.558.clone) | copy-start | bytes 28
  11.8 6.8 %collective-permute-start = (f32[19,1,8,128]{3,2,1,0:T(8,128)S(1)}, f32[19,1,8,128]{3,2,1,0:T(8,128)S(1)}, u32[]{:S(2)}, u32[]{:S(2)}) collective-permute-start(f32[19,1,8,128]{3,2,1,0:T(8,128)S(1)} %get-tuple-element.383), channel_id=1, source_target_pairs={{0,8},{8,16},{16,24},{24,0},{1,9},{9,17},{17,25},{25,1},{2,10},{10... | collective-permute-start | bytes 233480 | tf_op jit(solution)/shard_map/ppermute | solution.py:51
  14.5 5.0 %collective-permute-start.1 = (f32[19,1,8,128]{3,2,1,0:T(8,128)S(1)}, f32[19,1,8,128]{3,2,1,0:T(8,128)S(1)}, u32[]{:S(2)}, u32[]{:S(2)}) collective-permute-start(f32[19,1,8,128]{3,2,1,0:T(8,128)S(1)} %get-tuple-element.384), channel_id=1, source_target_pairs={{8,0},{16,8},{24,16},{0,24},{9,1},{17,9},{25,17},{1,25},{10,2},{18... | collective-permute-start | bytes 233480 | tf_op jit(solution)/shard_map/ppermute | solution.py:53
  19.7 1.4 %collective-permute-start.2 = (f32[19,10,1,128]{3,2,1,0:T(1,128)S(1)}, f32[19,10,1,128]{3,2,1,0:T(1,128)S(1)}, u32[]{:S(2)}, u32[]{:S(2)}) collective-permute-start(f32[19,10,1,128]{3,2,1,0:T(1,128)S(1)} %get-tuple-element.375), channel_id=1, source_target_pairs={{0,4},{4,0},{1,5},{5,1},{2,6},{6,2},{3,7},{7,3},{8,12},{12,8},{9,1... | collective-permute-start | bytes 291848 | tf_op jit(solution)/shard_map/ppermute | solution.py:51
  19.8 1.4 %collective-permute-start.3 = (f32[19,10,1,128]{3,2,1,0:T(1,128)S(1)}, f32[19,10,1,128]{3,2,1,0:T(1,128)S(1)}, u32[]{:S(2)}, u32[]{:S(2)}) collective-permute-start(f32[19,10,1,128]{3,2,1,0:T(1,128)S(1)} %get-tuple-element.376), channel_id=1, source_target_pairs={{4,0},{0,4},{5,1},{1,5},{6,2},{2,6},{7,3},{3,7},{12,8},{8,12},{13,... | collective-permute-start | bytes 291848 | tf_op jit(solution)/shard_map/ppermute | solution.py:53
  25.4 4.5 %copy-start.15 = (s32[2,8,128]{2,1,0:T(8,128)S(1)}, s32[2,8,128]{2,1,0:T(8,128)}, u32[]{:S(2)}) copy-start(s32[2,8,128]{2,1,0:T(8,128)} %param.55) | copy-start | bytes 24580
  25.4 5.6 %collective-permute-start.5 = (f32[19,10,10,1]{0,3,2,1:T(1,128)S(1)}, f32[19,10,10,1]{0,3,2,1:T(1,128)S(1)}, u32[]{:S(2)}, u32[]{:S(2)}) collective-permute-start(f32[19,10,10,1]{0,3,2,1:T(1,128)S(1)} %copy.55), channel_id=1, source_target_pairs={{1,0},{2,1},{3,2},{0,3},{5,4},{6,5},{7,6},{4,7},{9,8},{10,9},{11,1... | collective-permute-start | bytes 22808 | tf_op jit(solution)/shard_map/ppermute | solution.py:53
  29.8 5.9 %collective-permute-start.4 = (f32[19,10,10,1]{0,3,2,1:T(1,128)S(1)}, f32[19,10,10,1]{0,3,2,1:T(1,128)S(1)}, u32[]{:S(2)}, u32[]{:S(2)}) collective-permute-start(f32[19,10,10,1]{0,3,2,1:T(1,128)S(1)} %copy.53), channel_id=1, source_target_pairs={{0,1},{1,2},{2,3},{3,0},{4,5},{5,6},{6,7},{7,4},{8,9},{9,10},{10,1... | collective-permute-start | bytes 22808 | tf_op jit(solution)/shard_map/ppermute | solution.py:51
  29.9 11.0 %copy-start.10 = (pred[1,8,128]{2,1,0:T(8,128)(4,1)}, pred[1,8,128]{2,1,0:T(8,128)(4,1)S(1)}, u32[]{:S(2)}) copy-start(pred[1,8,128]{2,1,0:T(8,128)(4,1)S(1)} %get-tuple-element.317) | copy-start | bytes 3076
  39.4 1.4 %copy-start = (f32[19,10,10,1]{3,2,1,0:T(8,128)S(1)}, f32[19,10,10,1]{3,2,1,0:T(8,128)}, u32[]{:S(2)}) copy-start(f32[19,10,10,1]{3,2,1,0:T(8,128)} %copy.54) | copy-start | bytes 22804
  40.9 0.6 copy-start.12
  48.5 5.3 %collective-permute-start.6 = (f32[19,1,8,128]{3,2,1,0:T(8,128)S(1)}, f32[19,1,8,128]{3,2,1,0:T(8,128)S(1)}, u32[]{:S(2)}, u32[]{:S(2)}) collective-permute-start(f32[19,1,8,128]{3,2,1,0:T(8,128)S(1)} %get-tuple-element.382), channel_id=1, source_target_pairs={{0,8},{8,16},{16,24},{24,0},{1,9},{9,17},{17,25},{25,1},{2,10},{10... | collective-permute-start | bytes 233480 | tf_op jit(solution)/shard_map/ppermute | solution.py:51
  50.6 4.4 %collective-permute-start.7 = (f32[19,1,8,128]{3,2,1,0:T(8,128)S(1)}, f32[19,1,8,128]{3,2,1,0:T(8,128)S(1)}, u32[]{:S(2)}, u32[]{:S(2)}) collective-permute-start(f32[19,1,8,128]{3,2,1,0:T(8,128)S(1)} %get-tuple-element.381), channel_id=1, source_target_pairs={{8,0},{16,8},{24,16},{0,24},{9,1},{17,9},{25,17},{1,25},{10,2},{18... | collective-permute-start | bytes 233480 | tf_op jit(solution)/shard_map/ppermute | solution.py:53
  55.2 1.4 %collective-permute-start.8 = (f32[19,10,1,128]{3,2,1,0:T(1,128)S(1)}, f32[19,10,1,128]{3,2,1,0:T(1,128)S(1)}, u32[]{:S(2)}, u32[]{:S(2)}) collective-permute-start(f32[19,10,1,128]{3,2,1,0:T(1,128)S(1)} %get-tuple-element.371), channel_id=1, source_target_pairs={{0,4},{4,0},{1,5},{5,1},{2,6},{6,2},{3,7},{7,3},{8,12},{12,8},{9,1... | collective-permute-start | bytes 291848 | tf_op jit(solution)/shard_map/ppermute | solution.py:51
  55.2 1.4 %collective-permute-start.9 = (f32[19,10,1,128]{3,2,1,0:T(1,128)S(1)}, f32[19,10,1,128]{3,2,1,0:T(1,128)S(1)}, u32[]{:S(2)}, u32[]{:S(2)}) collective-permute-start(f32[19,10,1,128]{3,2,1,0:T(1,128)S(1)} %get-tuple-element.372), channel_id=1, source_target_pairs={{4,0},{0,4},{5,1},{1,5},{6,2},{2,6},{7,3},{3,7},{12,8},{8,12},{13,... | collective-permute-start | bytes 291848 | tf_op jit(solution)/shard_map/ppermute | solution.py:53
  60.8 10.4 %collective-permute-start.10 = (f32[19,10,10,1]{0,3,2,1:T(1,128)S(1)}, f32[19,10,10,1]{0,3,2,1:T(1,128)}, u32[]{:S(2)}, u32[]{:S(2)}) collective-permute-start(f32[19,10,10,1]{0,3,2,1:T(1,128)S(1)} %copy.57), channel_id=1, source_target_pairs={{0,1},{1,2},{2,3},{3,0},{4,5},{5,6},{6,7},{7,4},{8,9},{9,10},{10,1... | collective-permute-start | bytes 22808 | tf_op jit(solution)/shard_map/ppermute | solution.py:51
  61.6 5.8 %collective-permute-start.11 = (f32[19,10,10,1]{0,3,2,1:T(1,128)S(1)}, f32[19,10,10,1]{0,3,2,1:T(1,128)}, u32[]{:S(2)}, u32[]{:S(2)}) collective-permute-start(f32[19,10,10,1]{0,3,2,1:T(1,128)S(1)} %copy.59), channel_id=1, source_target_pairs={{1,0},{2,1},{3,2},{0,3},{5,4},{6,5},{7,6},{4,7},{9,8},{10,9},{11,1... | collective-permute-start | bytes 22808 | tf_op jit(solution)/shard_map/ppermute | solution.py:53
  69.8 0.7 copy-start.13
  71.2 0.6 copy-start.4
  75.3 1.5 %copy-start.1 = (f32[19,10,10,1]{3,2,1,0:T(8,128)S(1)}, f32[19,10,10,1]{3,2,1,0:T(8,128)}, u32[]{:S(2)}) copy-start(f32[19,10,10,1]{3,2,1,0:T(8,128)} %copy.58) | copy-start | bytes 22804
  75.3 1.5 %copy-start.11 = (pred[1,8,128]{2,1,0:T(8,128)(4,1)S(1)}, pred[1,8,128]{2,1,0:T(8,128)(4,1)}, u32[]{:S(2)}) copy-start(pred[1,8,128]{2,1,0:T(8,128)(4,1)} %copy-done.10) | copy-start | bytes 3076
  77.5 1.4 %copy-start.14 = (pred[1,8,128]{2,1,0:T(8,128)(4,1)S(1)}, pred[1,8,128]{2,1,0:T(8,128)(4,1)}, u32[]{:S(2)}) copy-start(pred[1,8,128]{2,1,0:T(8,128)(4,1)} %copy-done.12) | copy-start | bytes 3076
  78.9 1.5 %copy-start.5 = (f32[8,8,128]{2,1,0:T(8,128)S(1)}, f32[8,8,128]{2,1,0:T(8,128)}, u32[]{:S(2)}) copy-start(f32[8,8,128]{2,1,0:T(8,128)} %copy-done.4) | copy-start | bytes 98308
  78.9 1.5 %copy-start.7 = (s32[8,8,128]{2,1,0:T(8,128)S(1)}, s32[8,8,128]{2,1,0:T(8,128)}, u32[]{:S(2)}) copy-start(s32[8,8,128]{2,1,0:T(8,128)} %param.54) | copy-start | bytes 98308
  81.8 21.2 %copy-start.6 = (f32[1,8,8,128]{3,2,1,0:T(8,128)S(1)}, f32[1,8,8,128]{3,2,1,0:T(8,128)}, u32[]{:S(2)}) copy-start(f32[1,8,8,128]{3,2,1,0:T(8,128)} %get-tuple-element.273) | copy-start | bytes 98308
  81.8 21.3 %copy-start.9 = (f32[2,1,2,64]{3,2,1,0:T(2,128)S(1)}, f32[2,1,2,64]{3,2,1,0:T(2,128)}, u32[]{:S(2)}) copy-start(f32[2,1,2,64]{3,2,1,0:T(2,128)} %param.56) | copy-start | bytes 3076
  81.8 21.3 %copy-start.17 = (f32[2,1,2,64]{3,2,1,0:T(2,128)S(1)}, f32[2,1,2,64]{3,2,1,0:T(2,128)}, u32[]{:S(2)}) copy-start(f32[2,1,2,64]{3,2,1,0:T(2,128)} %param.57) | copy-start | bytes 3076
  81.8 21.3 %copy-start.18 = (f32[2,1,2,1]{3,2,1,0:T(2,128)S(1)}, f32[2,1,2,1]{3,2,1,0:T(2,128)}, u32[]{:S(2)}) copy-start(f32[2,1,2,1]{3,2,1,0:T(2,128)} %get-tuple-element.394) | copy-start | bytes 52
  81.8 21.3 %copy-start.19 = (f32[2,1,2,1]{3,2,1,0:T(2,128)S(1)}, f32[2,1,2,1]{3,2,1,0:T(2,128)}, u32[]{:S(2)}) copy-start(f32[2,1,2,1]{3,2,1,0:T(2,128)} %get-tuple-element.395) | copy-start | bytes 52
  81.9 21.3 %copy-start.20 = (f32[2,1,2,63]{3,2,1,0:T(2,128)S(1)}, f32[2,1,2,63]{3,2,1,0:T(2,128)}, u32[]{:S(2)}) copy-start(f32[2,1,2,63]{3,2,1,0:T(2,128)} %get-tuple-element.396) | copy-start | bytes 3028
  81.9 21.3 %copy-start.21 = (f32[2,1,2,63]{3,2,1,0:T(2,128)S(1)}, f32[2,1,2,63]{3,2,1,0:T(2,128)}, u32[]{:S(2)}) copy-start(f32[2,1,2,63]{3,2,1,0:T(2,128)} %get-tuple-element.397) | copy-start | bytes 3028
  81.9 21.3 %copy-start.22 = (f32[2,1,1,64]{3,2,1,0:T(1,128)S(1)}, f32[2,1,1,64]{3,2,1,0:T(1,128)}, u32[]{:S(2)}) copy-start(f32[2,1,1,64]{3,2,1,0:T(1,128)} %get-tuple-element.392) | copy-start | bytes 1540
  81.9 21.3 %copy-start.23 = (f32[2,1,1,64]{3,2,1,0:T(1,128)S(1)}, f32[2,1,1,64]{3,2,1,0:T(1,128)}, u32[]{:S(2)}) copy-start(f32[2,1,1,64]{3,2,1,0:T(1,128)} %get-tuple-element.393) | copy-start | bytes 1540
  81.9 21.3 %copy-start.25 = (f32[2]{0:T(128)S(1)}, f32[2]{0:T(128)}, u32[]{:S(2)}) copy-start(f32[2]{0:T(128)} %constant.557.clone) | copy-start | bytes 28
  81.9 21.3 %copy-start.27 = (f32[2]{0:T(128)S(1)}, f32[2]{0:T(128)}, u32[]{:S(2)}) copy-start(f32[2]{0:T(128)} %constant.558.clone) | copy-start | bytes 28
  81.9 21.3 %copy-start.28 = (f32[2]{0:T(128)S(1)}, f32[2]{0:T(128)}, u32[]{:S(2)}) copy-start(f32[2]{0:T(128)} %constant.555.clone) | copy-start | bytes 28
  81.9 21.3 %copy-start.29 = (f32[2]{0:T(128)S(1)}, f32[2]{0:T(128)}, u32[]{:S(2)}) copy-start(f32[2]{0:T(128)} %constant.556.clone) | copy-start | bytes 28
  103.1 1.5 %copy-start.3 = (f32[19,8,8,128]{3,2,1,0:T(8,128)}, f32[19,8,8,128]{3,2,1,0:T(8,128)S(1)}, u32[]{:S(2)}) copy-start(f32[19,8,8,128]{3,2,1,0:T(8,128)S(1)} %constant_dynamic-update-slice_fusion.38) | copy-start | bytes 1867780
where the time goes:
time: 106 us; the launch traced here: 105 us
  local copies, waits for them, and re-layouts  29.9 us (28%)
  other arithmetic  22.8 us (22%)
  starting transfers between devices  22.4 us (21%)
  blocking collectives  15.5 us (15%)
  waiting for transfers between devices  12.7 us (12%)
  between operations  1.35 us (1%)
    all_gather x1, blocking collectives, body(): coarse_vel = lax.all_gather(across, 'gx', axis=3, tiled=True)  13.6 us
    ppermute x7, starting transfers between devices, extended(): lax.ppermute(head, axis, [((i + 1) % count, i) for i in range(ends)])  11.8 us
    unnamed x35, other arithmetic  10.8 us
    ppermute x7, starting transfers between devices, extended(): lax.ppermute(tail, axis, [(i, (i + 1) % count) for i in range(ends)])  10.6 us
    ppermute x7, waiting for transfers between devices, extended(): lax.ppermute(tail, axis, [(i, (i + 1) % count) for i in range(ends)])  7.47 us
    unnamed x82, local copies, waits for them, and re-layouts  6.83 us
    slice x5, local copies, waits for them, and re-layouts, extended(): head = lax.slice_in_dim(cells, 0, width, axis=dim)  6.35 us
    ppermute x2, local copies, waits for them, and re-layouts, extended(): lax.ppermute(tail, axis, [(i, (i + 1) % count) for i in range(ends)])  6.09 us
  transfers between devices with their start and end apart: 14, of which 11 were waited for; matrix products, arithmetic and copies ran while one was open for 46% of the time, Pallas kernels for 0%

commit v1 on v0

v1 whole, which is shorter than its diff:
```python
import functools

import jax
import jax.numpy as jnp
from jax import lax
from jax.experimental import pallas as pl
from jax.experimental.pallas import tpu as pltpu
from jax.sharding import PartitionSpec as P

ITERS = 2
CELL = 8
MESH = pl.DeviceIdType.MESH

lattice = [
    (0, 0, 0),
    (1, 0, 0),
    (-1, 0, 0),
    (0, 1, 0),
    (0, -1, 0),
    (0, 0, 1),
    (0, 0, -1),
    (1, 1, 0),
    (-1, -1, 0),
    (1, -1, 0),
    (-1, 1, 0),
    (1, 0, 1),
    (-1, 0, -1),
    (1, 0, -1),
    (-1, 0, 1),
    (0, 1, 1),
    (0, -1, -1),
    (0, 1, -1),
    (0, -1, 1),
]
opposite = [0, 2, 1, 4, 3, 6, 5, 8, 7, 10, 9, 12, 11, 14, 13, 16, 15, 18, 17]
weights = [1.0 / 3.0] + [1.0 / 18.0] * 6 + [1.0 / 36.0] * 12
relax_rate = 1.25
base_density = 36.0
inlet_speed = 0.05
spread_base = (0.03, 0.06)
spread_length = 0.1
uptake_rate = (0.3, 0.6)
affinity = (2.0, 0.5)
phase_ratio = 0.5
feed_level = (1.0, 0.5)

GROUPS = [[[m for m in range(19) if lattice[m][d] == s] for s in (1, -1)] for d in range(3)]
ORDER = GROUPS[0][0] + GROUPS[0][1] + [m for m in range(19) if lattice[m][0] == 0]
SLOT = {m: i for i, m in enumerate(ORDER)}
ZY, ZX, YX = (7, 8, 9, 10), (11, 12, 13, 14), (15, 16, 17, 18)


def side(step):
    return 0 if step == 1 else 1


def moments(f):
    density = f[0]
    for member in range(1, 19):
        density = density + f[member]
    return density, momentum(f)


def momentum(f):
    flows = []
    for d in range(3):
        total = None
        for a, b in zip(GROUPS[d][0], [opposite[m] for m in GROUPS[d][0]]):
            part = f[a] - f[b]
            total = part if total is None else total + part
        flows.append(total)
    return flows


def balance(scale, velocity, members):
    square = velocity[0] * velocity[0] + velocity[1] * velocity[1] + velocity[2] * velocity[2]
    base = 1.0 - 1.5 * square
    cache, result = {}, {}
    for w in set(weights[m] for m in members):
        cache[w] = scale * w
    for m in members:
        if m == 0:
            result[m] = cache[weights[0]] * base
            continue
        key = min(m, opposite[m])
        if ("pair", key) not in cache:
            along = None
            for d in range(3):
                step = lattice[key][d]
                if step:
                    term = velocity[d]
                    if along is None:
                        along = term if step == 1 else -term
                    else:
                        along = along + term if step == 1 else along - term
            cache[("pair", key)] = (base + 4.5 * along * along, 3.0 * along)
        even, odd = cache[("pair", key)]
        result[m] = cache[weights[m]] * (even + odd if m == key else even - odd)
    return result


def collide(f, solid):
    density, flows = moments(f)
    inverse = 1.0 / density
    velocity = [flow * inverse for flow in flows]
    feq = balance(relax_rate * density, velocity, range(19))
    post = [
        jnp.where(solid, f[opposite[m]], (1.0 - relax_rate) * f[m] + feq[m]) for m in range(19)
    ]
    return post, velocity


def kernel(sizes, *refs):
    nz, ny, nx = sizes
    (pop_hbm, solid_hbm, ports_hbm, conc_hbm, load_hbm, out, new_conc, new_load,
     pops, solid, ports, conc, load, post0, post1, speed, ypack, xpack,
     zrecv, yrecv, xrecv, zyrecv, zxrecv, yxrecv, corner, near, wrapped,
     sent_v, all_v, vel, load_sem, send_sem, recv_sem, near_sem, vsend, vrecv) = refs
    D, H, W = solid.shape
    ncy, ncx = conc.shape[2:]
    gz, gy, gx = lax.axis_index("gz"), lax.axis_index("gy"), lax.axis_index("gx")
    is_first, is_last = gz == 0, gz == nz - 1
    has_up, has_down = gz < nz - 1, gz > 0

    small = [
        pltpu.make_async_copy(a, b, load_sem.at[D + i])
        for i, (a, b) in enumerate(
            ((solid_hbm, solid), (ports_hbm, ports), (conc_hbm, conc), (load_hbm, load)))
    ]
    small[0].start()

    def plane_in(z):
        return pltpu.make_async_copy(pop_hbm.at[:, z], pops.at[:, z], load_sem.at[z])

    for z in range(D):
        plane_in(z).start()
    for copy in small[1:]:
        copy.start()

    def at(offset):
        dz, dy, dx = offset
        return {"gz": gz + dz, "gy": lax.rem(gy + dy + ny, ny), "gx": lax.rem(gx + dx + nx, nx)}

    flat = [(0, dy, dx) for dy in range(ny) for dx in range(nx) if dy or dx]
    cross = sorted({(dy % ny, dx % nx) for dy, dx in ((0, 0), (1, 0), (-1, 0), (0, 1), (0, -1))})
    barrier = pltpu.get_barrier_semaphore()

    def greet(offsets):
        for offset in offsets:
            pl.semaphore_signal(barrier, inc=1, device_id=at(offset), device_id_type=MESH)

    greet(flat)

    @pl.when(has_up)
    def _():
        greet([(1, dy, dx) for dy, dx in cross])

    @pl.when(has_down)
    def _():
        greet([(-1, dy, dx) for dy, dx in cross])

    lane = lax.broadcasted_iota(jnp.int32, (H, W), 1)
    row = lax.broadcasted_iota(jnp.int32, (H, W), 0)
    edge_lane = [lane == 0, lane == W - 1]
    edge_row = [row == 0, row == H - 1]
    first_mask = jnp.full((H, W), gz, jnp.int32) == 0
    last_mask = jnp.full((H, W), gz, jnp.int32) == nz - 1

    def rolled(x, step, axis):
        size = x.shape[axis]
        return pltpu.roll(x, step % size, axis)

    def blank(s):
        for it in range(ITERS):
            zrecv[it, s] = jnp.zeros(zrecv.shape[2:], jnp.float32)
            for at_member in range(4):
                if side(lattice[ZY[at_member]][0]) == s:
                    zyrecv[it, at_member] = jnp.zeros((H, W), jnp.float32)
                if side(lattice[ZX[at_member]][0]) == s:
                    zxrecv[it, at_member] = jnp.zeros((H, W), jnp.float32)

    for i in range(4):
        if i != 0:
            small[i].wait()

    @pl.when(is_first)
    def _():
        blank(0)
        for s in range(2):
            near[0, s] = jnp.full(near.shape[2:], feed_level[s], jnp.float32)

    @pl.when(is_last)
    def _():
        blank(1)
        near[1] = conc[...]

    posts = (post0, post1)

    def store_post(it, z, post, packs):
        where = posts[it]
        for m in range(19):
            where[SLOT[m], z] = post[m]
        for s in range(2):
            for i, m in enumerate(GROUPS[1][s]):
                edge = post[m][H - 1 :, :] if s == 0 else post[m][:1, :]
                ypack[it, s, i, pl.ds(z, 1), :] = edge
        new = []
        for s in range(2):
            acc = packs[s]
            for i, m in enumerate(GROUPS[2][s]):
                k = i * D + z
                acc = jnp.where(lane == k, pltpu.roll(post[m], k + 1 - s, 1), acc)
            new.append(acc)
        return tuple(new)

    def finish(it, packs):
        for s in range(2):
            xpack[it, s] = packs[s]

    def exchange(it):
        where = posts[it]
        moves = []
        for m in ZX:
            z = D - 1 if lattice[m][0] == 1 else 0
            moves.append((where.at[SLOT[m], z], zxrecv.at[it, m - ZX[0]], lattice[m]))
        for s in range(2):
            moves.append((xpack.at[it, s], xrecv.at[it, s], (0, 0, 1 - 2 * s)))
        for m in YX:
            s = side(lattice[m][1])
            moves.append((ypack.at[it, s, GROUPS[1][s].index(m)], yxrecv.at[it, m - YX[0]], lattice[m]))
        for m in ZY:
            z = D - 1 if lattice[m][0] == 1 else 0
            moves.append((where.at[SLOT[m], z], zyrecv.at[it, m - ZY[0]], lattice[m]))
        for s in range(2):
            z = D - 1 if s == 0 else 0
            moves.append((where.at[pl.ds(5 * s, 5), z], zrecv.at[it, s], (1 - 2 * s, 0, 0)))
        for s in range(2):
            moves.append((ypack.at[it, s], yrecv.at[it, s], (0, 1 - 2 * s, 0)))
        copies = {-1: [], 0: [], 1: []}
        for i, (src, dst, offset) in enumerate(moves):
            copies[offset[0]].append(
                pltpu.make_async_remote_copy(
                    src_ref=src, dst_ref=dst, send_sem=send_sem.at[it, i],
                    recv_sem=recv_sem.at[it, i], device_id=at(offset), device_id_type=MESH))
        return copies

    def run(copies, method, incoming=False):
        conds = {1: has_down, -1: has_up} if incoming else {1: has_up, -1: has_down}
        for dz in (1, -1):
            @pl.when(conds[dz])
            def _():
                for copy in copies[dz]:
                    getattr(copy, method)()
        for copy in copies[0]:
            getattr(copy, method)()

    small[0].wait()
    zero = jnp.zeros((H, W), jnp.float32)

    def first_plane(z, packs):
        plane_in(z).wait()
        f = [pops[m, z] for m in range(19)]
        post, velocity = collide(f, solid[z] == 1)
        if isinstance(z, int):
            for d in range(3):
                speed[0, d] = velocity[d]
        return store_post(0, z, post, packs)

    packs = lax.fori_loop(0, D - 1, first_plane, (zero, zero))
    packs = first_plane(D - 1, packs)
    finish(0, packs)

    up_down = jnp.where(has_up, len(cross), 0) + jnp.where(has_down, len(cross), 0)
    pl.semaphore_wait(barrier, len(flat) + up_down)

    moves0 = exchange(0)
    run(moves0, "start")
    ends = {1: [], -1: [], 0: []}
    for s in range(2):
        dz = 1 - 2 * s
        ends[dz].append(
            pltpu.make_async_remote_copy(
                src_ref=conc, dst_ref=near.at[s], send_sem=near_sem.at[0, s],
                recv_sem=near_sem.at[1, s], device_id=at((dz, 0, 0)), device_id_type=MESH))
    run(ends, "start")

    def arrive(it, copies):
        run(copies, "wait_recv", incoming=True)
        for m in YX:
            _, cy, cx = lattice[m]
            s = side(cy)
            own = rolled(yrecv[it, s, GROUPS[1][s].index(m)], cx, 1)
            far = rolled(yxrecv[it, m - YX[0]], cx, 1)
            corner[it, m - YX[0]] = jnp.where(edge_lane[side(cx)], far, own)

    def stream(it, z, place):
        where = posts[it]
        f = []
        for m in range(19):
            cz, cy, cx = lattice[m]
            beyond = (cz == 1 and place == "low") or (cz == -1 and place == "high")
            if beyond:
                s = side(cz)
                v = zrecv[it, s, GROUPS[0][s].index(m)]
            else:
                v = where[SLOT[m], z - cz]
            if cx:
                s = side(cx)
                if beyond:
                    column = rolled(zxrecv[it, m - ZX[0]], cx, 1)
                else:
                    k = GROUPS[2][s].index(m) * D + z - cz
                    column = pltpu.roll(xrecv[it, s], W - k if s == 0 else W - 1 - k, 1) \
                        if not (isinstance(k, int) and k == 0 and s == 0) else xrecv[it, s]
                v = jnp.where(edge_lane[s], column, rolled(v, cx, 1))
            if cy:
                s = side(cy)
                if beyond:
                    r = H - 1 if s == 0 else 0
                    line = zyrecv[it, m - ZY[0], r : r + 1, :]
                elif cx:
                    line = corner[it, m - YX[0], pl.ds(z, 1), :]
                else:
                    line = yrecv[it, s, GROUPS[1][s].index(m), pl.ds(z - cz, 1), :]
                v = jnp.where(edge_row[s], jnp.broadcast_to(line, (H, W)), rolled(v, cy, 0))
            f.append(v)
        if place == "low":
            inflow = equilibrium_at_inlet()
            opened = ports[0] == 1
            for m in GROUPS[0][0]:
                back = where[SLOT[opposite[m]], 0]
                f[m] = jnp.where(first_mask, jnp.where(opened, inflow[m], back), f[m])
        if place == "high":
            velocity = [speed[it, d] for d in range(3)]
            outflow = balance(base_density, velocity, GROUPS[0][1])
            opened = ports[1] == 1
            for m in GROUPS[0][1]:
                back = where[SLOT[opposite[m]], D - 1]
                f[m] = jnp.where(last_mask, jnp.where(opened, outflow[m], back), f[m])
        return f

    def planes(step, carry):
        carry = step(0, "low", carry)
        carry = lax.fori_loop(1, D - 1, lambda z, c: step(z, "mid", c), carry)
        return step(D - 1, "high", carry)

    arrive(0, moves0)

    def second_plane(z, place, packs):
        f = stream(0, z, place)
        post, velocity = collide(f, solid[z] == 1)
        if place == "high":
            for d in range(3):
                speed[1, d] = velocity[d]
        return store_post(1, z, post, packs)

    finish(1, planes(second_plane, (zero, zero)))
    moves1 = exchange(1)
    run(moves1, "start")

    run(ends, "wait_recv", incoming=True)
    source = lax.broadcasted_iota(jnp.int32, (ncx, ncx), 0)
    target = lax.broadcasted_iota(jnp.int32, (ncx, ncx), 1)
    ahead = jnp.where(target == ncx - 1, 0, target + 1)
    behind = jnp.where(target == 0, ncx - 1, target - 1)
    take_after = (source == ahead).astype(jnp.float32)
    take_before = (source == behind).astype(jnp.float32)

    def exact_dot(a, b):
        return jnp.dot(a, b, precision=lax.Precision.HIGHEST, preferred_element_type=jnp.float32)

    diffs = []
    for s in range(2):
        c = conc[s, 0]
        wrapped[s, 1 : ncy + 1, :] = c
        wrapped[s, 0:1, :] = conc[s, 0, ncy - 1 : ncy, :]
        wrapped[s, ncy + 1 : ncy + 2, :] = conc[s, 0, 0:1, :]
        pairs = [
            (near[0, s, 0], near[1, s, 0]),
            (wrapped[s, 0:ncy, :], wrapped[s, 2 : ncy + 2, :]),
            (exact_dot(c, take_before), exact_dot(c, take_after)),
        ]
        curvature = sum(b + a - 2.0 * c for b, a in pairs)
        rate = uptake_rate[s] * (affinity[s] * c - load[s, 0])
        new_load[s, 0] = load[s, 0] + rate
        diffs.append((c - phase_ratio * rate + spread_base[s] * curvature, curvature,
                      [(c - b, a - c) for b, a in pairs]))

    arrive(1, moves1)

    def last_plane(z, place, totals):
        f = stream(1, z, place)
        for m in range(19):
            out[m, z] = f[m]
        pore = solid[z] == 0
        return tuple(t + jnp.where(pore, flow, 0.0) for t, flow in zip(totals, momentum(f)))

    totals = planes(last_plane, (zero, zero, zero))
    sums = zero
    for d in range(3):
        line = jnp.sum(totals[d], axis=0, keepdims=True)
        sums = jnp.where(row == d, jnp.broadcast_to(line, (H, W)), sums)
    wide = sent_v.shape[1]
    voxel = lax.broadcasted_iota(jnp.int32, (W, wide), 0)
    cell = lax.broadcasted_iota(jnp.int32, (W, wide), 1) - gx * (W // CELL)
    pick = ((voxel >= cell * CELL) & (voxel < cell * CELL + CELL)).astype(jnp.float32)
    sent_v[...] = exact_dot(sums, pick) * (1.0 / (CELL * CELL * CELL * base_density))
    tell = [
        pltpu.make_async_remote_copy(
            src_ref=sent_v, dst_ref=all_v.at[gy, gx], send_sem=vsend.at[i],
            recv_sem=vrecv.at[i], device_id=at(offset), device_id_type=MESH)
        for i, offset in enumerate(flat)
    ]
    for copy in tell:
        copy.start()
    all_v[gy, gx] = sent_v[...]
    run(moves0, "wait_send")
    run(moves1, "wait_send")
    run(ends, "wait_send")
    for copy in tell:
        copy.wait_recv()

    for y in range(ny):
        total = all_v[y, 0]
        for x in range(1, nx):
            total = total + all_v[y, x]
        for d in range(3):
            vel[d, y : y + 1, :] = total[d : d + 1, :]
    courant = [CELL * vel[d][:, :ncx] for d in range(3)]
    reach = jnp.abs(courant[0]) + jnp.abs(courant[1]) + jnp.abs(courant[2])
    for s in range(2):
        value, curvature, steps = diffs[s]
        for d in range(3):
            low, high = steps[d]
            value = value - jnp.maximum(courant[d], 0.0) * low - jnp.minimum(courant[d], 0.0) * high
        new_conc[s, 0] = value + spread_length * reach * curvature
    for copy in tell:
        copy.wait_send()


def equilibrium_at_inlet():
    result = {}
    for m in GROUPS[0][0]:
        along = inlet_speed
        result[m] = weights[m] * base_density * (
            1.0 + 3.0 * along + 4.5 * along * along - 1.5 * inlet_speed * inlet_speed)
    return result


def solution(mesh):
    sizes = tuple(mesh.shape[a] for a in ("gz", "gy", "gx"))
    nz, ny, nx = sizes

    def body(populations, solid, ports, concentration, loaded):
        D, H, W = solid.shape
        ncy, ncx = concentration.shape[2:]
        assert D == CELL and H == CELL and W % 128 == 0 and 5 * D <= W
        wide = -(-ncx // 128) * 128
        f32 = jnp.float32
        tile = (H, W)
        anywhere = pl.BlockSpec(memory_space=pl.ANY)
        inside = pl.BlockSpec(memory_space=pltpu.VMEM)
        return pl.pallas_call(
            functools.partial(kernel, sizes),
            out_shape=(
                jax.ShapeDtypeStruct(populations.shape, f32),
                jax.ShapeDtypeStruct(concentration.shape, f32),
                jax.ShapeDtypeStruct(loaded.shape, f32),
            ),
            in_specs=[anywhere] * 5,
            out_specs=(inside,) * 3,
            scratch_shapes=[
                pltpu.VMEM(populations.shape, f32),
                pltpu.VMEM(solid.shape, jnp.int32),
                pltpu.VMEM(ports.shape, jnp.int32),
                pltpu.VMEM(concentration.shape, f32),
                pltpu.VMEM(loaded.shape, f32),
                pltpu.VMEM((19, D) + tile, f32),
                pltpu.VMEM((19, D) + tile, f32),
                pltpu.VMEM((ITERS, 3) + tile, f32),
                pltpu.VMEM((ITERS, 2, 5, D, W), f32),
                pltpu.VMEM((ITERS, 2) + tile, f32),
                pltpu.VMEM((ITERS, 2, 5) + tile, f32),
                pltpu.VMEM((ITERS, 2, 5, D, W), f32),
                pltpu.VMEM((ITERS, 2) + tile, f32),
                pltpu.VMEM((ITERS, 4) + tile, f32),
                pltpu.VMEM((ITERS, 4) + tile, f32),
                pltpu.VMEM((ITERS, 4, D, W), f32),
                pltpu.VMEM((ITERS, 4, D, W), f32),
                pltpu.VMEM((2,) + concentration.shape, f32),
                pltpu.VMEM((2, ncy + 2, ncx), f32),
                pltpu.VMEM((8, wide), f32),
                pltpu.VMEM((ny, nx, 8, wide), f32),
                pltpu.VMEM((3, ncy, wide), f32),
                pltpu.SemaphoreType.DMA((D + 4,)),
                pltpu.SemaphoreType.DMA((ITERS, 18)),
                pltpu.SemaphoreType.DMA((ITERS, 18)),
                pltpu.SemaphoreType.DMA((2, 2)),
                pltpu.SemaphoreType.DMA((ny * nx - 1,)),
                pltpu.SemaphoreType.DMA((ny * nx - 1,)),
            ],
            compiler_params=pltpu.CompilerParams(collective_id=0, has_side_effects=True),
        )(populations, solid, ports, concentration, loaded)

    placed = (
        P(None, "gz", "gy", "gx"),
        P("gz", "gy", "gx"),
        P(None, "gy", "gx"),
        P(None, "gz", None, None),
        P(None, "gz", None, None),
    )
    return jax.shard_map(
        body,
        mesh=mesh,
        in_specs=placed,
        out_specs=(P(None, "gz", "gy", "gx"), P(None, "gz", None, None), P(None, "gz", None, None)),
        check_vma=False,
    )
```

time: 106 us -> 26.2 us (0.25); the launches traced: 105 us -> 26 us
  local copies, waits for them, and re-layouts: 29.9 us -> 3.2 us
  other arithmetic: 22.8 us -> 0 us
  starting transfers between devices: 22.4 us -> 0 us
  Pallas kernels: 0 us -> 22.2 us
  blocking collectives: 15.5 us -> 0 us
  waiting for transfers between devices: 12.7 us -> 0 us
    ppermute x14 -> x0, starting transfers between devices: 22.4 us -> none  [the longest x7 11.8 us: extended(): lax.ppermute(head, axis, [((i + 1) % count, i) for i in range(ends)])]
    pallas_call x0 -> x1, Pallas kernels: none -> 22.2 us  [body(): pl.pallas_call(functools.partial(kernel, sizes), out_shape=(jax.ShapeDtyp...]
    all_gather x2 -> x0, blocking collectives: 15.5 us -> none  [the longest x1 13.6 us: body(): coarse_vel = lax.all_gather(across, 'gx', axis=3, tiled=True)]
    ppermute x14 -> x0, waiting for transfers between devices: 12.7 us -> none  [the longest x7 7.47 us: extended(): lax.ppermute(tail, axis, [(i, (i + 1) % count) for i in range(ends)])]
    slice x12 -> x0, local copies, waits for them, and re-layouts: 11.4 us -> none  [the longest x5 6.35 us: extended(): head = lax.slice_in_dim(cells, 0, width, axis=dim)]
    unnamed x35 -> x0, other arithmetic: 10.8 us -> none
    ppermute x4 -> x0, local copies, waits for them, and re-layouts: 10.1 us -> none  [the longest x2 6.09 us: extended(): lax.ppermute(tail, axis, [(i, (i + 1) % count) for i in range(ends)])]
    scatter x13 -> x0, other arithmetic: 4.67 us -> none  [the longest x8 3.08 us: close_ends(): result[member].at[-1].set(jnp.where(last_dev, entering, result[member][-1]))]
  transfers between devices with their start and end apart: 14 -> 0, of which waited for: 11 -> 0; matrix products, arithmetic and copies ran while one was open for 46% -> 0% of each run, Pallas kernels for 0% -> 0%
where the time goes in v1:
time: 26.2 us; the launch traced here: 26 us
  Pallas kernels  22.2 us (85%)
  local copies, waits for them, and re-layouts  3.2 us (12%)
  between operations  0.65 us (2%)
    pallas_call x1, Pallas kernels, body(): pl.pallas_call(functools.partial(kernel, sizes), out_shape=(jax.ShapeDtyp...  22.2 us
    unnamed x7, local copies, waits for them, and re-layouts  3.2 us

profile of v1, /device:TPU:0, one launch (start us, length us, event | category | flops | bytes accessed | tf_op | source)
XLA Modules:
  0.0 26.0 jit_solution(8256682958826332590)
XLA Ops:
  0.6 22.2 %shard_map.76 = (f32[19,8,8,128]{3,2,1,0:T(8,128)}, f32[2,1,2,64]{3,2,1,0:T(2,128)}, f32[2,1,2,64]{3,2,1,0:T(2,128)}) custom-call(f32[19,8,8,128]{3,2,1,0:T(8,128)} %refs_0_.1, s32[8,8,128]{2,1,0:T(8,128)} %refs_1_.1, s32[2,8,128]{2,1,0:T(8,128)} %refs_2_.1, f32[2,1,2,64]{3,2,1,0:T(2,128)} %refs_3_.1, f32[2,1,2,64]{3,2,1,0:T(2,128)} %refs_4_.1), custom_call_target="tpu_custom_call" | custom-call | tf_op jit(solution)/shard_map/pallas_call | solution.py:463
  22.8 0.0 copy-start.1
  22.8 2.0 %copy.11 = f32[19,8,8,128]{3,2,1,0:T(8,128)} copy(f32[19,8,8,128]{3,2,1,0:T(8,128)} %get-tuple-element.6) | data formatting | bytes 1245184
  24.8 0.0 copy-done.1
  24.8 0.0 copy-start
  24.8 0.6 %copy.12 = f32[2,1,2,64]{3,2,1,0:T(2,128)} copy(f32[2,1,2,64]{3,2,1,0:T(2,128)S(1)} %copy-done.1) | data formatting | bytes 2048
  25.4 0.1 copy-done
  25.4 0.6 %copy.13 = f32[2,1,2,64]{3,2,1,0:T(2,128)} copy(f32[2,1,2,64]{3,2,1,0:T(2,128)S(1)} %copy-done) | data formatting | bytes 2048
Async XLA Ops:
  22.8 2.0 %copy-start.1 = (f32[2,1,2,64]{3,2,1,0:T(2,128)S(1)}, f32[2,1,2,64]{3,2,1,0:T(2,128)}, u32[]{:S(2)}) copy-start(f32[2,1,2,64]{3,2,1,0:T(2,128)} %get-tuple-element.7) | copy-start | bytes 3076
  24.8 0.7 %copy-start = (f32[2,1,2,64]{3,2,1,0:T(2,128)S(1)}, f32[2,1,2,64]{3,2,1,0:T(2,128)}, u32[]{:S(2)}) copy-start(f32[2,1,2,64]{3,2,1,0:T(2,128)} %get-tuple-element.8) | copy-start | bytes 3076

commit v2 on v1

--- a/solution.py
+++ b/solution.py
@@ -438,6 +438,14 @@
         copy.wait_send()
 
 
+def hand_out(*refs):
+    copies = [pltpu.make_async_copy(refs[i], refs[3 + i], refs[6].at[i]) for i in range(3)]
+    for copy in copies:
+        copy.start()
+    for copy in copies:
+        copy.wait()
+
+
 def equilibrium_at_inlet():
     result = {}
     for m in GROUPS[0][0]:
@@ -460,13 +468,10 @@
         tile = (H, W)
         anywhere = pl.BlockSpec(memory_space=pl.ANY)
         inside = pl.BlockSpec(memory_space=pltpu.VMEM)
-        return pl.pallas_call(
+        results = (populations, concentration, loaded)
+        made = pl.pallas_call(
             functools.partial(kernel, sizes),
-            out_shape=(
-                jax.ShapeDtypeStruct(populations.shape, f32),
-                jax.ShapeDtypeStruct(concentration.shape, f32),
-                jax.ShapeDtypeStruct(loaded.shape, f32),
-            ),
+            out_shape=tuple(pltpu.VMEM(a.shape, f32) for a in results),
             in_specs=[anywhere] * 5,
             out_specs=(inside,) * 3,
             scratch_shapes=[
@@ -501,6 +506,13 @@
             ],
             compiler_params=pltpu.CompilerParams(collective_id=0, has_side_effects=True),
         )(populations, solid, ports, concentration, loaded)
+        return pl.pallas_call(
+            hand_out,
+            out_shape=tuple(jax.ShapeDtypeStruct(a.shape, f32) for a in results),
+            in_specs=[inside] * 3,
+            out_specs=(anywhere,) * 3,
+            scratch_shapes=[pltpu.SemaphoreType.DMA((3,))],
+        )(*[pltpu.with_memory_space_constraint(a, pltpu.VMEM) for a in made])
 
     placed = (
         P(None, "gz", "gy", "gx"),

time: 26.2 us -> 23 us (0.88)
  local copies, waits for them, and re-layouts: 3.2 us -> 0 us
    unnamed x7 -> x0, local copies, waits for them, and re-layouts: 3.2 us -> none
    pallas_call x1 -> x2, Pallas kernels: 22.2 us -> 22.2 us  [the longest x1 21.3 us: body(): pl.pallas_call(functools.partial(kernel, sizes), out_shape=tuple((pltpu.V...]
where the time goes in v2:
time: 23 us; the launch traced here: 22.8 us
  Pallas kernels  22.2 us (97%)
  between operations  0.64 us (3%)
    pallas_call x1, Pallas kernels, body(): pl.pallas_call(functools.partial(kernel, sizes), out_shape=tuple((pltpu.V...  21.3 us
    pallas_call x1, Pallas kernels, body(): pl.pallas_call(hand_out, out_shape=tuple((jax.ShapeDtypeStruct(a.shape, f...  0.86 us

profile of v2, /device:TPU:0, one launch (start us, length us, event | category | flops | bytes accessed | tf_op | source)
XLA Modules:
  0.0 22.8 jit_solution(5367903477508054185)
XLA Ops:
  0.6 21.3 %shard_map.76 = (f32[19,8,8,128]{3,2,1,0:T(8,128)S(1)}, f32[2,1,2,64]{3,2,1,0:T(2,128)S(1)}, f32[2,1,2,64]{3,2,1,0:T(2,128)S(1)}) custom-call(f32[19,8,8,128]{3,2,1,0:T(8,128)} %refs_0_.1, s32[8,8,128]{2,1,0:T(8,128)} %refs_1_.1, s32[2,8,128]{2,1,0:T(8,128)} %refs_2_.1, f32[2,1,2,64]{3,2,1,0:T(2,128)} %refs_3_.1, f32[2,1,2,64]{3,2,1,0:T(2,128)} %refs_4_.1), custom_call_target="tpu_custom_call" | custom-call | tf_op jit(solution)/shard_map/pallas_call | solution.py:472
  22.0 0.9 %shard_map.77 = (f32[19,8,8,128]{3,2,1,0:T(8,128)}, f32[2,1,2,64]{3,2,1,0:T(2,128)}, f32[2,1,2,64]{3,2,1,0:T(2,128)}) custom-call(f32[19,8,8,128]{3,2,1,0:T(8,128)S(1)} %get-tuple-element.6.refs_0_, f32[2,1,2,64]{3,2,1,0:T(2,128)S(1)} %get-tuple-element.7.refs_1_, f32[2,1,2,64]{3,2,1,0:T(2,128)S(1)} %get-tuple-element.8.refs_2_), custom_call_target="tpu_custom_call" | custom-call | tf_op jit(solution)/shard_map/pallas_call | solution.py:509

commit v3 on v2

--- a/solution.py
+++ b/solution.py
@@ -114,7 +114,7 @@
     nz, ny, nx = sizes
     (pop_hbm, solid_hbm, ports_hbm, conc_hbm, load_hbm, out, new_conc, new_load,
      pops, solid, ports, conc, load, post0, post1, speed, ypack, xpack,
-     zrecv, yrecv, xrecv, zyrecv, zxrecv, yxrecv, corner, near, wrapped,
+     zyline, zrecv, yrecv, xrecv, zyrecv, zxrecv, yxrecv, corner, near, wrapped,
      sent_v, all_v, vel, load_sem, send_sem, recv_sem, near_sem, vsend, vrecv) = refs
     D, H, W = solid.shape
     ncy, ncx = conc.shape[2:]
@@ -175,7 +175,7 @@
             zrecv[it, s] = jnp.zeros(zrecv.shape[2:], jnp.float32)
             for at_member in range(4):
                 if side(lattice[ZY[at_member]][0]) == s:
-                    zyrecv[it, at_member] = jnp.zeros((H, W), jnp.float32)
+                    zyrecv[it, at_member] = jnp.zeros((1, W), jnp.float32)
                 if side(lattice[ZX[at_member]][0]) == s:
                     zxrecv[it, at_member] = jnp.zeros((H, W), jnp.float32)
 
@@ -204,6 +204,11 @@
             for i, m in enumerate(GROUPS[1][s]):
                 edge = post[m][H - 1 :, :] if s == 0 else post[m][:1, :]
                 ypack[it, s, i, pl.ds(z, 1), :] = edge
+        if isinstance(z, int):
+            for m in ZY:
+                cz, cy, _ = lattice[m]
+                if z == (D - 1 if cz == 1 else 0):
+                    zyline[it, m - ZY[0]] = post[m][H - 1 :, :] if cy == 1 else post[m][:1, :]
         new = []
         for s in range(2):
             acc = packs[s]
@@ -220,17 +225,16 @@
     def exchange(it):
         where = posts[it]
         moves = []
+        for s in range(2):
+            moves.append((xpack.at[it, s], xrecv.at[it, s], (0, 0, 1 - 2 * s)))
         for m in ZX:
             z = D - 1 if lattice[m][0] == 1 else 0
             moves.append((where.at[SLOT[m], z], zxrecv.at[it, m - ZX[0]], lattice[m]))
-        for s in range(2):
-            moves.append((xpack.at[it, s], xrecv.at[it, s], (0, 0, 1 - 2 * s)))
         for m in YX:
             s = side(lattice[m][1])
             moves.append((ypack.at[it, s, GROUPS[1][s].index(m)], yxrecv.at[it, m - YX[0]], lattice[m]))
         for m in ZY:
-            z = D - 1 if lattice[m][0] == 1 else 0
-            moves.append((where.at[SLOT[m], z], zyrecv.at[it, m - ZY[0]], lattice[m]))
+            moves.append((zyline.at[it, m - ZY[0]], zyrecv.at[it, m - ZY[0]], lattice[m]))
         for s in range(2):
             z = D - 1 if s == 0 else 0
             moves.append((where.at[pl.ds(5 * s, 5), z], zrecv.at[it, s], (1 - 2 * s, 0, 0)))
@@ -246,13 +250,17 @@
 
     def run(copies, method, incoming=False):
         conds = {1: has_down, -1: has_up} if incoming else {1: has_up, -1: has_down}
+        for copy in copies.get(0, ()):
+            getattr(copy, method)()
         for dz in (1, -1):
-            @pl.when(conds[dz])
-            def _():
-                for copy in copies[dz]:
-                    getattr(copy, method)()
-        for copy in copies[0]:
-            getattr(copy, method)()
+            if copies.get(dz):
+                @pl.when(conds[dz])
+                def _():
+                    for copy in copies[dz]:
+                        getattr(copy, method)()
+
+    def cross_arrive(copies):
+        run({1: copies[1], -1: copies[-1]}, "wait_recv", incoming=True)
 
     small[0].wait()
     zero = jnp.zeros((H, W), jnp.float32)
@@ -261,12 +269,13 @@
         plane_in(z).wait()
         f = [pops[m, z] for m in range(19)]
         post, velocity = collide(f, solid[z] == 1)
-        if isinstance(z, int):
+        if isinstance(z, int) and z == D - 1:
             for d in range(3):
                 speed[0, d] = velocity[d]
         return store_post(0, z, post, packs)
 
-    packs = lax.fori_loop(0, D - 1, first_plane, (zero, zero))
+    packs = first_plane(0, (zero, zero))
+    packs = lax.fori_loop(1, D - 1, first_plane, packs)
     packs = first_plane(D - 1, packs)
     finish(0, packs)
 
@@ -285,7 +294,7 @@
     run(ends, "start")
 
     def arrive(it, copies):
-        run(copies, "wait_recv", incoming=True)
+        run({0: copies[0]}, "wait_recv")
         for m in YX:
             _, cy, cx = lattice[m]
             s = side(cy)
@@ -316,8 +325,7 @@
             if cy:
                 s = side(cy)
                 if beyond:
-                    r = H - 1 if s == 0 else 0
-                    line = zyrecv[it, m - ZY[0], r : r + 1, :]
+                    line = zyrecv[it, m - ZY[0]]
                 elif cx:
                     line = corner[it, m - YX[0], pl.ds(z, 1), :]
                 else:
@@ -339,9 +347,10 @@
                 f[m] = jnp.where(last_mask, jnp.where(opened, outflow[m], back), f[m])
         return f
 
-    def planes(step, carry):
+    def planes(step, carry, crossing):
+        carry = lax.fori_loop(1, D - 1, lambda z, c: step(z, "mid", c), carry)
+        crossing()
         carry = step(0, "low", carry)
-        carry = lax.fori_loop(1, D - 1, lambda z, c: step(z, "mid", c), carry)
         return step(D - 1, "high", carry)
 
     arrive(0, moves0)
@@ -354,7 +363,7 @@
                 speed[1, d] = velocity[d]
         return store_post(1, z, post, packs)
 
-    finish(1, planes(second_plane, (zero, zero)))
+    finish(1, planes(second_plane, (zero, zero), lambda: cross_arrive(moves0)))
     moves1 = exchange(1)
     run(moves1, "start")
 
@@ -395,16 +404,18 @@
         pore = solid[z] == 0
         return tuple(t + jnp.where(pore, flow, 0.0) for t, flow in zip(totals, momentum(f)))
 
-    totals = planes(last_plane, (zero, zero, zero))
+    totals = planes(last_plane, (zero, zero, zero), lambda: cross_arrive(moves1))
     sums = zero
     for d in range(3):
         line = jnp.sum(totals[d], axis=0, keepdims=True)
         sums = jnp.where(row == d, jnp.broadcast_to(line, (H, W)), sums)
-    wide = sent_v.shape[1]
+    wide = sent_v.shape[2]
     voxel = lax.broadcasted_iota(jnp.int32, (W, wide), 0)
     cell = lax.broadcasted_iota(jnp.int32, (W, wide), 1) - gx * (W // CELL)
     pick = ((voxel >= cell * CELL) & (voxel < cell * CELL + CELL)).astype(jnp.float32)
-    sent_v[...] = exact_dot(sums, pick) * (1.0 / (CELL * CELL * CELL * base_density))
+    mine = exact_dot(sums, pick) * (1.0 / (CELL * CELL * CELL * base_density))
+    for d in range(3):
+        sent_v[d] = mine[d : d + 1, :]
     tell = [
         pltpu.make_async_remote_copy(
             src_ref=sent_v, dst_ref=all_v.at[gy, gx], send_sem=vsend.at[i],
@@ -425,7 +436,7 @@
         for x in range(1, nx):
             total = total + all_v[y, x]
         for d in range(3):
-            vel[d, y : y + 1, :] = total[d : d + 1, :]
+            vel[d, y : y + 1, :] = total[d]
     courant = [CELL * vel[d][:, :ncx] for d in range(3)]
     reach = jnp.abs(courant[0]) + jnp.abs(courant[1]) + jnp.abs(courant[2])
     for s in range(2):
@@ -485,17 +496,18 @@
                 pltpu.VMEM((ITERS, 3) + tile, f32),
                 pltpu.VMEM((ITERS, 2, 5, D, W), f32),
                 pltpu.VMEM((ITERS, 2) + tile, f32),
+                pltpu.VMEM((ITERS, 4, 1, W), f32),
                 pltpu.VMEM((ITERS, 2, 5) + tile, f32),
                 pltpu.VMEM((ITERS, 2, 5, D, W), f32),
                 pltpu.VMEM((ITERS, 2) + tile, f32),
-                pltpu.VMEM((ITERS, 4) + tile, f32),
+                pltpu.VMEM((ITERS, 4, 1, W), f32),
                 pltpu.VMEM((ITERS, 4) + tile, f32),
                 pltpu.VMEM((ITERS, 4, D, W), f32),
                 pltpu.VMEM((ITERS, 4, D, W), f32),
                 pltpu.VMEM((2,) + concentration.shape, f32),
                 pltpu.VMEM((2, ncy + 2, ncx), f32),
-                pltpu.VMEM((8, wide), f32),
-                pltpu.VMEM((ny, nx, 8, wide), f32),
+                pltpu.VMEM((3, 1, wide), f32),
+                pltpu.VMEM((ny, nx, 3, 1, wide), f32),
                 pltpu.VMEM((3, ncy, wide), f32),
                 pltpu.SemaphoreType.DMA((D + 4,)),
                 pltpu.SemaphoreType.DMA((ITERS, 18)),

time: 23 us -> 21.3 us (0.926)
  Pallas kernels: 22.2 us -> 20.5 us
    pallas_call x1, Pallas kernels: 21.3 us -> 19.7 us  [body(): pl.pallas_call(functools.partial(kernel, sizes), out_shape=tuple((pltpu.V...]
where the time goes in v3:
time: 21.3 us; the launch traced here: 21.2 us
  Pallas kernels  20.5 us (96%)
  between operations  0.64 us (3%)
    pallas_call x1, Pallas kernels, body(): pl.pallas_call(functools.partial(kernel, sizes), out_shape=tuple((pltpu.V...  19.7 us
    pallas_call x1, Pallas kernels, body(): pl.pallas_call(hand_out, out_shape=tuple((jax.ShapeDtypeStruct(a.shape, f...  0.86 us

profile of v3, /device:TPU:0, one launch (start us, length us, event | category | flops | bytes accessed | tf_op | source)
XLA Modules:
  0.0 21.2 jit_solution(4369780197654082321)
XLA Ops:
  0.6 19.7 %shard_map.76 = (f32[19,8,8,128]{3,2,1,0:T(8,128)S(1)}, f32[2,1,2,64]{3,2,1,0:T(2,128)S(1)}, f32[2,1,2,64]{3,2,1,0:T(2,128)S(1)}) custom-call(f32[19,8,8,128]{3,2,1,0:T(8,128)} %refs_0_.1, s32[8,8,128]{2,1,0:T(8,128)} %refs_1_.1, s32[2,8,128]{2,1,0:T(8,128)} %refs_2_.1, f32[2,1,2,64]{3,2,1,0:T(2,128)} %refs_3_.1, f32[2,1,2,64]{3,2,1,0:T(2,128)} %refs_4_.1), custom_call_target="tpu_custom_call" | custom-call | tf_op jit(solution)/shard_map/pallas_call | solution.py:483
  20.3 0.9 %shard_map.77 = (f32[19,8,8,128]{3,2,1,0:T(8,128)}, f32[2,1,2,64]{3,2,1,0:T(2,128)}, f32[2,1,2,64]{3,2,1,0:T(2,128)}) custom-call(f32[19,8,8,128]{3,2,1,0:T(8,128)S(1)} %get-tuple-element.6.refs_0_, f32[2,1,2,64]{3,2,1,0:T(2,128)S(1)} %get-tuple-element.7.refs_1_, f32[2,1,2,64]{3,2,1,0:T(2,128)S(1)} %get-tuple-element.8.refs_2_), custom_call_target="tpu_custom_call" | custom-call | tf_op jit(solution)/shard_map/pallas_call | solution.py:521

commit v4 on v3

--- a/solution.py
+++ b/solution.py
@@ -283,7 +283,8 @@
     pl.semaphore_wait(barrier, len(flat) + up_down)
 
     moves0 = exchange(0)
-    run(moves0, "start")
+    run({1: moves0[1], -1: moves0[-1]}, "start")
+    run({0: moves0[0]}, "start")
     ends = {1: [], -1: [], 0: []}
     for s in range(2):
         dz = 1 - 2 * s
@@ -294,7 +295,25 @@
     run(ends, "start")
 
     def arrive(it, copies):
-        run({0: copies[0]}, "wait_recv")
+        run({0: copies[0][-2:]}, "wait_recv")
+
+        def prepare(z, carry):
+            for m in range(19):
+                cz, cy, cx = lattice[m]
+                v = posts[it][SLOT[m], z - cz]
+                if cx:
+                    v = rolled(v, cx, 1)
+                if cy:
+                    v = rolled(v, cy, 0)
+                    if not cx:
+                        s = side(cy)
+                        line = yrecv[it, s, GROUPS[1][s].index(m), pl.ds(z - cz, 1), :]
+                        v = jnp.where(edge_row[s], jnp.broadcast_to(line, (H, W)), v)
+                pops[m, z] = v
+            return carry
+
+        lax.fori_loop(1, D - 1, prepare, 0)
+        run({0: copies[0][:-2]}, "wait_recv")
         for m in YX:
             _, cy, cx = lattice[m]
             s = side(cy)
@@ -305,6 +324,22 @@
     def stream(it, z, place):
         where = posts[it]
         f = []
+        if place == "mid":
+            for m in range(19):
+                cz, cy, cx = lattice[m]
+                v = pops[m, z]
+                if cx:
+                    s = side(cx)
+                    k = GROUPS[2][s].index(m) * D + z - cz
+                    column = pltpu.roll(xrecv[it, s], W - k if s == 0 else W - 1 - k, 1)
+                    if cy:
+                        column = rolled(column, cy, 0)
+                    v = jnp.where(edge_lane[s], column, v)
+                    if cy:
+                        line = corner[it, m - YX[0], pl.ds(z, 1), :]
+                        v = jnp.where(edge_row[side(cy)], jnp.broadcast_to(line, (H, W)), v)
+                f.append(v)
+            return f
         for m in range(19):
             cz, cy, cx = lattice[m]
             beyond = (cz == 1 and place == "low") or (cz == -1 and place == "high")
@@ -355,17 +390,22 @@
 
     arrive(0, moves0)
 
+    moves1 = exchange(1)
+
     def second_plane(z, place, packs):
         f = stream(0, z, place)
         post, velocity = collide(f, solid[z] == 1)
         if place == "high":
             for d in range(3):
                 speed[1, d] = velocity[d]
-        return store_post(1, z, post, packs)
+        packs = store_post(1, z, post, packs)
+        if place != "mid":
+            dz = -1 if place == "low" else 1
+            run({dz: moves1[dz]}, "start")
+        return packs
 
     finish(1, planes(second_plane, (zero, zero), lambda: cross_arrive(moves0)))
-    moves1 = exchange(1)
-    run(moves1, "start")
+    run({0: moves1[0]}, "start")
 
     run(ends, "wait_recv", incoming=True)
     source = lax.broadcasted_iota(jnp.int32, (ncx, ncx), 0)

time: 21.3 us -> 21.1 us (level)
    pallas_call x1, Pallas kernels: 19.7 us -> 19.4 us  [body(): pl.pallas_call(functools.partial(kernel, sizes), out_shape=tuple((pltpu.V...]
where the time goes in v4:
time: 21.1 us; the launch traced here: 20.9 us
  Pallas kernels  20.3 us (96%)
  between operations  0.64 us (3%)
    pallas_call x1, Pallas kernels, body(): pl.pallas_call(functools.partial(kernel, sizes), out_shape=tuple((pltpu.V...  19.4 us
    pallas_call x1, Pallas kernels, body(): pl.pallas_call(hand_out, out_shape=tuple((jax.ShapeDtypeStruct(a.shape, f...  0.86 us

profile of v4, /device:TPU:0, one launch (start us, length us, event | category | flops | bytes accessed | tf_op | source)
XLA Modules:
  0.0 20.9 jit_solution(7982365899711243755)
XLA Ops:
  0.6 19.4 %shard_map.76 = (f32[19,8,8,128]{3,2,1,0:T(8,128)S(1)}, f32[2,1,2,64]{3,2,1,0:T(2,128)S(1)}, f32[2,1,2,64]{3,2,1,0:T(2,128)S(1)}) custom-call(f32[19,8,8,128]{3,2,1,0:T(8,128)} %refs_0_.1, s32[8,8,128]{2,1,0:T(8,128)} %refs_1_.1, s32[2,8,128]{2,1,0:T(8,128)} %refs_2_.1, f32[2,1,2,64]{3,2,1,0:T(2,128)} %refs_3_.1, f32[2,1,2,64]{3,2,1,0:T(2,128)} %refs_4_.1), custom_call_target="tpu_custom_call" | custom-call | tf_op jit(solution)/shard_map/pallas_call | solution.py:523
  20.0 0.9 %shard_map.77 = (f32[19,8,8,128]{3,2,1,0:T(8,128)}, f32[2,1,2,64]{3,2,1,0:T(2,128)}, f32[2,1,2,64]{3,2,1,0:T(2,128)}) custom-call(f32[19,8,8,128]{3,2,1,0:T(8,128)S(1)} %get-tuple-element.6.refs_0_, f32[2,1,2,64]{3,2,1,0:T(2,128)S(1)} %get-tuple-element.7.refs_1_, f32[2,1,2,64]{3,2,1,0:T(2,128)S(1)} %get-tuple-element.8.refs_2_), custom_call_target="tpu_custom_call" | custom-call | tf_op jit(solution)/shard_map/pallas_call | solution.py:561
